TPU v7x, 32 devices: a whole 2x2x4 slice. The times are simulated.
32 devices in a mesh: ctx: 8 (over z, y), head: 4 (over x, core).
Axes of the slice: x: 2, y: 2, z: 4, core: 2. Of those that a mesh axis runs over, the one named last changes fastest.
Arguments:
- tokens: bfloat16 [4096, 2048], P('ctx', 'head'), may hold values from -6 to 6
- value_weight: bfloat16 [2048, 4096], P('ctx', 'head'), may hold values from -0.125 to 0.125
- queries: bfloat16 [4096, 128], P('ctx'), may hold values from -2.390625 to 2.390625
- key_vectors: bfloat16 [4096, 128], P('ctx'), may hold values from -2.390625 to 2.390625
- level_weight: float32 [13, 64, 4096], P(None, 'head', 'ctx'), may hold values from 0.2 to 1
Outputs:
- attended: bfloat16 [4096, 4096], P('ctx', 'head')
All inputs are finite; a program needn't handle non-finite values.
Results may differ from a plain program's by a relative error of at most 0.006.
Values may be sent and summed in bfloat16 or wider, within the bound.
No kernel may reach another device: no remote copies, remote signals or barrier semaphores. Data moves between devices by JAX's collectives and lax.ppermute only.
A program may use at most 64 MiB of HBM per device.

v0:
```python
import jax
import jax.numpy as jnp
from jax import lax
from jax.sharding import PartitionSpec as P


def from_partner(block, axis, distance):
    count = lax.axis_size(axis)
    route = []
    for low in range(count):
        high = low | 1 << distance
        if high != low and high < count:
            route += [(low, high), (high, low)]
    return lax.ppermute(block, axis, route)


def body(tokens, value_weight, queries, key_vectors, level_weight):
    features = lax.all_gather(tokens, "head", axis=1, tiled=True)
    length = features.shape[0]
    width_local = value_weight.shape[1]
    head_local = level_weight.shape[1]
    head_size = width_local // head_local
    state_rows = queries.shape[1]
    stretch_bits = length.bit_length() - 1
    ctx_count = lax.axis_size("ctx")
    dev_bits = ctx_count.bit_length() - 1
    values = jnp.dot(
        features,
        lax.all_gather(value_weight, "ctx", axis=0, tiled=True),
        preferred_element_type=jnp.float32,
    ).astype(jnp.bfloat16)
    tile_len = min(128, length)
    tile_count = length // tile_len
    tile_bits = tile_len.bit_length() - 1
    q_tiles = queries.reshape(tile_count, tile_len, state_rows)
    k_tiles = key_vectors.reshape(tile_count, tile_len, state_rows)
    v_tiles = values.reshape(tile_count, tile_len, width_local)
    tile_scores = jnp.einsum(
        "bin,bjn->bij", q_tiles, k_tiles, preferred_element_type=jnp.float32
    ).astype(jnp.bfloat16)
    row_pos = lax.broadcasted_iota(jnp.int32, (tile_len, tile_len), 0)
    col_pos = lax.broadcasted_iota(jnp.int32, (tile_len, tile_len), 1)
    differ = jnp.bitwise_xor(row_pos, col_pos)
    pair_level = jnp.zeros((tile_len, tile_len), jnp.int32)
    for bit_num in range(tile_bits):
        pair_level = pair_level + (jnp.right_shift(differ, bit_num) > 0).astype(jnp.int32)
    causal = col_pos <= row_pos
    result = jnp.zeros((length, head_local, head_size), jnp.float32)
    for level_num in range(0, tile_bits + 1):
        scale = 1.0 if level_num == 0 else 2.0 ** (-(level_num - 1) / 2.0)
        chosen = causal & (pair_level == level_num)
        masked = jnp.where(chosen[None], tile_scores, jnp.zeros_like(tile_scores))
        mixed = jnp.einsum("bij,bjc->bic", masked, v_tiles, preferred_element_type=jnp.float32)
        weights = level_weight[level_num].T * scale
        result = result + weights[..., None] * mixed.reshape(length, head_local, head_size)
    for level_num in range(tile_bits + 1, stretch_bits + 1):
        half_len = 2 ** (level_num - 1)
        groups = length // (2 * half_len)
        scale = 2.0 ** (-(level_num - 1) / 2.0)
        q_right = queries.reshape(groups, 2, half_len, state_rows)[:, 1]
        k_left = key_vectors.reshape(groups, 2, half_len, state_rows)[:, 0]
        v_left = values.reshape(groups, 2, half_len, width_local)[:, 0]
        scores = jnp.einsum(
            "bin,bjn->bij", q_right, k_left, preferred_element_type=jnp.float32
        ).astype(jnp.bfloat16)
        mixed = jnp.einsum("bij,bjc->bic", scores, v_left, preferred_element_type=jnp.float32)
        weights = level_weight[level_num].T.reshape(groups, 2, half_len, head_local)[:, 1] * scale
        addend = weights[..., None] * mixed.reshape(groups, half_len, head_local, head_size)
        result = result.reshape(groups, 2, half_len, head_local, head_size).at[:, 1].add(addend)
        result = result.reshape(length, head_local, head_size)
    state = jnp.einsum("tn,tc->nc", key_vectors, values, preferred_element_type=jnp.float32)
    my_index = lax.axis_index("ctx")
    running = state
    level_states = []
    for section_bit in range(dev_bits):
        partner = from_partner(running, "ctx", section_bit)
        is_right = my_index // 2**section_bit % 2 == 1
        level_states.append(jnp.where(is_right, partner, jnp.zeros_like(partner)))
        running = running + partner
    for section_bit in range(dev_bits):
        level_num = stretch_bits + 1 + section_bit
        scale = 2.0 ** (-(level_num - 1) / 2.0)
        state_high = level_states[section_bit].astype(jnp.bfloat16)
        state_low = (level_states[section_bit] - state_high.astype(jnp.float32)).astype(
            jnp.bfloat16
        )
        reading = jnp.dot(queries, state_high, preferred_element_type=jnp.float32)
        reading = reading + jnp.dot(queries, state_low, preferred_element_type=jnp.float32)
        weights = level_weight[level_num].T * scale
        result = result + weights[..., None] * reading.reshape(length, head_local, head_size)
    return result.reshape(length, width_local).astype(jnp.bfloat16)


def solution(mesh):
    return jax.shard_map(
        body,
        mesh=mesh,
        in_specs=(
            P("ctx", "head"),
            P("ctx", "head"),
            P("ctx", None),
            P("ctx", None),
            P(None, "head", "ctx"),
        ),
        out_specs=P("ctx", "head"),
        check_vma=False,
    )
```

profile of v0, /device:TPU:0, one launch (start us, length us, event | category | flops | bytes accessed | tf_op | source)
XLA Modules:
  0.0 205.0 jit_solution(3942225557572144632)
XLA Ops:
  8.1 1.6 multiply_bitcast_fusion.2
  21.2 13.0 %all-gather.3.cloned.1.call-done = bf16[512,2048]{1,0:T(8,128)(2,1)} async-done(((bf16[512,512]{1,0:T(8,128)(2,1)}), bf16[512,2048]{1,0:T(8,128)(2,1)}) %all-gather.3.cloned.1.call-update) | async-done | bytes 2097168 | tf_op jit(solution)/shard_map/all_gather | solution.py:18
  34.2 75.0 %all-gather.5.cloned.1.call-done = bf16[2048,1024]{1,0:T(8,128)(2,1)} async-done(((bf16[256,1024]{1,0:T(8,128)(2,1)}), bf16[2048,1024]{1,0:T(8,128)(2,1)}) %all-gather.5.cloned.1.call-update) | async-done | bytes 4194320 | tf_op jit(solution)/shard_map/all_gather | solution.py:29
  109.2 5.1 %convolution_convert_fusion = bf16[512,1024]{1,0:T(8,128)(2,1)S(1)} fusion(bf16[512,2048]{1,0:T(8,128)(2,1)} %all-gather.3.cloned.1.call-done, bf16[2048,1024]{1,0:T(8,128)(2,1)} %all-gather.5.cloned.1.call-done), kind=kOutput, calls=%fused_computation.8 | convolution fusion | flops 2148007936 | bytes 7340032 | tf_op jit(solution)/shard_map/dot_general | solution.py:27
  114.3 1.3 convolution_bitcast_fusion
  115.6 1.2 fusion.37
  116.9 1.9 fusion.35
  118.8 1.8 fusion.33
  120.6 1.9 fusion.31
  122.5 1.9 fusion.29
  124.4 1.9 fusion.27
  126.3 1.9 fusion.41
  128.2 1.9 fusion.39
  130.1 1.4 fusion.8
  131.5 7.9 %multiply_add_fusion = f32[2,2,128,16,64]{2,4,3,1,0:T(8,128)S(1)} fusion(f32[2,2,128,16,64]{2,4,3,1,0:T(8,128)} %bitcast.204, f32[2,2,128,16,64]{2,4,3,1,0:T(8,128)} %bitcast.203, f32[2,2,128,16,64]{2,4,3,1,0:T(8,128)} %bitcast.202, f32[2,2,128,16,64]{2,4,3,1,0:T(8,128)} %bitcast.201, f32[2,2,128,16,64]{2,4,3,1,0:T(8,128)} %bitcast.200, ...), kind=kLoop, calls=%fused_computation.7 | loop fusion | flops 7864320 | bytes 19136512 | tf_op jit(solution)/shard_map/add | solution.py:55
  139.8 3.2 %copy.41 = f32[2,2,128,16,64]{2,1,4,3,0:T(2,128)} copy(f32[2,2,128,16,64]{2,4,3,1,0:T(8,128)S(1)} %fusion.9) | data formatting | bytes 4194304 | tf_op jit(solution)/shard_map/scatter-add | solution.py:69
  142.9 2.9 %reshape_reshape.3 = f32[1,2,256,16,64]{2,4,3,1,0:T(8,128)S(1)} reshape(f32[2,2,128,16,64]{2,1,4,3,0:T(2,128)} %copy.41) | data formatting | bytes 4194304 | tf_op jit(solution)/shard_map/reshape;reshape | solution.py:69
  147.3 1.2 copy.43
  149.1 1.6 copy.44
  150.9 7.8 %collective-permute-done = f32[128,1024]{0,1:T(8,128)} collective-permute-done((f32[128,1024]{0,1:T(8,128)}, f32[128,1024]{0,1:T(8,128)}, u32[]{:S(2)}, u32[]{:S(2)}) %collective-permute-start) | collective-permute-done | bytes 524320 | tf_op jit(solution)/shard_map/ppermute | solution.py:14
  161.4 10.0 %collective-permute-done.1 = f32[128,1024]{0,1:T(8,128)S(1)} collective-permute-done((f32[128,1024]{0,1:T(8,128)S(1)}, f32[128,1024]{0,1:T(8,128)S(1)}, u32[]{:S(2)}, u32[]{:S(2)}) %collective-permute-start.1) | collective-permute-done | bytes 524320 | tf_op jit(solution)/shard_map/ppermute | solution.py:14
  171.5 3.0 %collective-permute-start.2 = (f32[128,1024]{0,1:T(8,128)S(1)}, f32[128,1024]{0,1:T(8,128)S(1)}, u32[]{:S(2)}, u32[]{:S(2)}) collective-permute-start(f32[128,1024]{0,1:T(8,128)S(1)} %add.368), channel_id=1, source_target_pairs={{0,16},{16,0},{4,20},{20,4},{8,24},{24,8},{12,28},{28,12},{1,17},{... | collective-permute-start | bytes 1572872 | tf_op jit(solution)/shard_map/ppermute | solution.py:14
  175.4 20.2 %collective-permute-done.2 = f32[128,1024]{0,1:T(8,128)S(1)} collective-permute-done((f32[128,1024]{0,1:T(8,128)S(1)}, f32[128,1024]{0,1:T(8,128)S(1)}, u32[]{:S(2)}, u32[]{:S(2)}) %collective-permute-start.2) | collective-permute-done | bytes 524320 | tf_op jit(solution)/shard_map/ppermute | solution.py:14
  196.9 1.3 copy.45
  (79 shorter events, 20.3 us)
Async XLA Ops:
  6.5 14.5 %copy-start = (bf16[512,128]{1,0:T(8,128)(2,1)S(1)}, bf16[512,128]{1,0:T(8,128)(2,1)}, u32[]{:S(2)}) copy-start(bf16[512,128]{1,0:T(8,128)(2,1)} %param.11) | copy-start | bytes 393220
  6.5 14.5 %copy-start.3 = (bf16[512,128]{1,0:T(8,128)(2,1)S(1)}, bf16[512,128]{1,0:T(8,128)(2,1)}, u32[]{:S(2)}) copy-start(bf16[512,128]{1,0:T(8,128)(2,1)} %param.12) | copy-start | bytes 393220
  6.5 27.7 %all-gather.3.cloned.1.call-start = ((), (), s32[]{:S(2)}) async-start(), calls=%async_computation | async-start | bytes 2621440 | tf_op jit(solution)/shard_map/all_gather | solution.py:18
  7.3 101.9 %all-gather.5.cloned.1.call-start = ((), (), s32[]{:S(2)}) async-start(), calls=%async_computation.1 | async-start | bytes 4718592 | tf_op jit(solution)/shard_map/all_gather | solution.py:29
  114.3 2.5 %copy-start.14 = (pred[128,128]{1,0:T(8,128)(4,1)S(1)}, pred[128,128]{1,0:T(8,128)(4,1)}, u32[]{:S(2)}) copy-start(pred[128,128]{1,0:T(8,128)(4,1)} %fusion.62) | copy-start | bytes 49156
  116.9 1.9 copy-start.13
  118.8 1.9 copy-start.12
  120.6 1.9 copy-start.11
  122.5 1.9 copy-start.10
  124.4 1.9 copy-start.9
  126.3 1.9 copy-start.8
  131.5 7.9 %copy-start.1 = (f32[2,128,1024]{1,2,0:T(8,128)S(1)}, f32[2,128,1024]{1,2,0:T(8,128)}, u32[]{:S(2)}) copy-start(f32[2,128,1024]{1,2,0:T(8,128)} %fusion.8) | copy-start | bytes 3145732
  131.5 7.9 %copy-start.7 = (f32[2,128,16]{1,2,0:T(8,128)S(1)}, f32[2,128,16]{1,2,0:T(8,128)}, u32[]{:S(2)}) copy-start(f32[2,128,16]{1,2,0:T(8,128)} %fusion.82) | copy-start | bytes 49156
  145.9 12.8 %collective-permute-start = (f32[128,1024]{0,1:T(8,128)}, f32[128,1024]{0,1:T(8,128)}, u32[]{:S(2)}, u32[]{:S(2)}) collective-permute-start(f32[128,1024]{0,1:T(8,128)} %convolution_bitcast_fusion), channel_id=1, source_target_pairs={{0,4},{4,0},{8,12},{12,8},{16,20},{20,16},{24,28},{28,24},{1,5},{5... | collective-permute-start | bytes 1572872 | tf_op jit(solution)/shard_map/ppermute | solution.py:14
  150.7 8.0 %copy-start.2 = (f32[128,1024]{0,1:T(8,128)S(1)}, f32[128,1024]{0,1:T(8,128)}, u32[]{:S(2)}) copy-start(f32[128,1024]{0,1:T(8,128)} %convolution_bitcast_fusion) | copy-start | bytes 1572868
  159.8 11.7 %collective-permute-start.1 = (f32[128,1024]{0,1:T(8,128)S(1)}, f32[128,1024]{0,1:T(8,128)S(1)}, u32[]{:S(2)}, u32[]{:S(2)}) collective-permute-start(f32[128,1024]{0,1:T(8,128)S(1)} %add.363), channel_id=1, source_target_pairs={{0,8},{8,0},{4,12},{12,4},{16,24},{24,16},{20,28},{28,20},{1,9},{9... | collective-permute-start | bytes 1572872 | tf_op jit(solution)/shard_map/ppermute | solution.py:14
  171.5 24.0 %collective-permute-start.2 = (f32[128,1024]{0,1:T(8,128)S(1)}, f32[128,1024]{0,1:T(8,128)S(1)}, u32[]{:S(2)}, u32[]{:S(2)}) collective-permute-start(f32[128,1024]{0,1:T(8,128)S(1)} %add.368), channel_id=1, source_target_pairs={{0,16},{16,0},{4,20},{20,4},{8,24},{24,8},{12,28},{28,12},{1,17},{... | collective-permute-start | bytes 1572872 | tf_op jit(solution)/shard_map/ppermute | solution.py:14
  174.9 21.1 %copy-start.4 = (f32[512,16]{0,1:T(8,128)S(1)}, f32[512,16]{0,1:T(8,128)}, u32[]{:S(2)}) copy-start(f32[512,16]{0,1:T(8,128)} %get-tuple-element.29) | copy-start | bytes 98308
  174.9 21.1 %copy-start.5 = (f32[512,16]{0,1:T(8,128)S(1)}, f32[512,16]{0,1:T(8,128)}, u32[]{:S(2)}) copy-start(f32[512,16]{0,1:T(8,128)} %get-tuple-element.40) | copy-start | bytes 98308
  175.0 21.1 %copy-start.6 = (f32[512,16]{0,1:T(8,128)S(1)}, f32[512,16]{0,1:T(8,128)}, u32[]{:S(2)}) copy-start(f32[512,16]{0,1:T(8,128)} %get-tuple-element.41) | copy-start | bytes 98308
Sparse Core Ops, SparseCore 0:
  8.9 25.2 all-gather.2
  36.3 72.7 all-gather.4
where the time goes:
time: 205 us
  waiting for transfers between devices  127 us (62%)
  matrix products  26 us (13%)
  other arithmetic  17.1 us (8%)
  local copies, waits for them, and re-layouts  16.5 us (8%)
  between operations  13.7 us (7%)
  starting transfers between devices  4.38 us (2%)
    all_gather x1, waiting for transfers between devices, body(): lax.all_gather(value_weight, 'ctx', axis=0, tiled=True)  75 us
    ppermute x3, waiting for transfers between devices, from_partner(): return lax.ppermute(block, axis, route)  38 us
    dot_general x8, matrix products, body(): jnp.einsum('bij,bjc->bic', masked, v_tiles, preferred_element_type=jnp.fl...  14.4 us
    all_gather x1, waiting for transfers between devices, body(): features = lax.all_gather(tokens, 'head', axis=1, tiled=True)  13 us
    add x1, other arithmetic, body(): result + weights[..., None] * mixed.reshape(length, head_local, head_size)  7.87 us
    and x8, other arithmetic, body(): chosen = causal & (pair_level == level_num)  5.44 us
    dot_general x1, matrix products, body(): jnp.dot(features, lax.all_gather(value_weight, 'ctx', axis=0, tiled=True)...  5.15 us
    mul x16, local copies, waits for them, and re-layouts, body(): weights[..., None] * mixed.reshape(length, head_local, head_size)  5.08 us
  transfers between devices with their start and end apart: 5, of which 5 were waited for; matrix products, arithmetic and copies ran while one was open for 9% of the time, Pallas kernels for 0%

commit v1 on v0

--- a/solution.py
+++ b/solution.py
@@ -2,6 +2,16 @@
 import jax.numpy as jnp
 from jax import lax
 from jax.sharding import PartitionSpec as P
+
+
+def gather_by_hops(x, mesh_axis, d):
+    size = lax.axis_size(mesh_axis)
+    current, blocks = (x, [x])
+    for _ in range(size - 1):
+        current = lax.ppermute(current, mesh_axis, [(i, (i + 1) % size) for i in range(size)])
+        blocks.insert(0, current)
+    line = jnp.concatenate(blocks, axis=d)
+    return jnp.roll(line, (lax.axis_index(mesh_axis) + 1) * x.shape[d], axis=d)
 
 
 def from_partner(block, axis, distance):
@@ -15,7 +25,7 @@
 
 
 def body(tokens, value_weight, queries, key_vectors, level_weight):
-    features = lax.all_gather(tokens, "head", axis=1, tiled=True)
+    features = gather_by_hops(tokens, "head", 1)
     length = features.shape[0]
     width_local = value_weight.shape[1]
     head_local = level_weight.shape[1]

time: 205 us -> 181 us (0.88)
  waiting for transfers between devices: 127 us -> 93 us
  local copies, waits for them, and re-layouts: 16.5 us -> 23.7 us
  starting transfers between devices: 4.38 us -> 7.49 us
    all_gather x1, waiting for transfers between devices: 75 us -> 43 us  [body(): lax.all_gather(value_weight, 'ctx', axis=0, tiled=True)]
    all_gather x1 -> x0, waiting for transfers between devices: 13 us -> none  [body(): features = lax.all_gather(tokens, 'head', axis=1, tiled=True)]
    ppermute x0 -> x3, waiting for transfers between devices: none -> 11.3 us  [gather_by_hops(): lax.ppermute(current, mesh_axis, [(i, (i + 1) % size) for i in range(size)])]
    unnamed x31 -> x42, local copies, waits for them, and re-layouts: 0.23 us -> 6.57 us
    ppermute x0 -> x3, starting transfers between devices: none -> 3.14 us  [gather_by_hops(): lax.ppermute(current, mesh_axis, [(i, (i + 1) % size) for i in range(size)])]
  transfers between devices with their start and end apart: 5 -> 7, of which waited for: 5 -> 6; matrix products, arithmetic and copies ran while one was open for 9% -> 15% of each run, Pallas kernels for 0% -> 0%
where the time goes in v1:
time: 181 us; the launch traced here: 180 us
  waiting for transfers between devices  93 us (51%)
  matrix products  25.3 us (14%)
  local copies, waits for them, and re-layouts  23.7 us (13%)
  other arithmetic  17 us (9%)
  between operations  13.7 us (8%)
  starting transfers between devices  7.49 us (4%)
    all_gather x1, waiting for transfers between devices, body(): lax.all_gather(value_weight, 'ctx', axis=0, tiled=True)  43 us
    ppermute x3, waiting for transfers between devices, from_partner(): return lax.ppermute(block, axis, route)  38 us
    dot_general x8, matrix products, body(): jnp.einsum('bij,bjc->bic', masked, v_tiles, preferred_element_type=jnp.fl...  13.7 us
    ppermute x3, waiting for transfers between devices, gather_by_hops(): lax.ppermute(current, mesh_axis, [(i, (i + 1) % size) for i in range(size)])  11.3 us
    add x1, other arithmetic, body(): result + weights[..., None] * mixed.reshape(length, head_local, head_size)  7.87 us
    unnamed x42, local copies, waits for them, and re-layouts  6.57 us
    and x8, other arithmetic, body(): chosen = causal & (pair_level == level_num)  5.44 us
    dot_general x1, matrix products, body(): jnp.dot(features, lax.all_gather(value_weight, 'ctx', axis=0, tiled=True)...  5.16 us
  transfers between devices with their start and end apart: 7, of which 6 were waited for; matrix products, arithmetic and copies ran while one was open for 15% of the time, Pallas kernels for 0%

profile of v1, /device:TPU:0, one launch (start us, length us, event | category | flops | bytes accessed | tf_op | source)
XLA Modules:
  0.0 180.2 jit_solution(7843981701105963360)
XLA Ops:
  7.8 1.6 multiply_bitcast_fusion.2
  17.4 2.6 %collective-permute-start.1 = (bf16[512,512]{1,0:T(8,128)(2,1)S(1)}, bf16[512,512]{1,0:T(8,128)(2,1)S(1)}, u32[]{:S(2)}, u32[]{:S(2)}) collective-permute-start(bf16[512,512]{1,0:T(8,128)(2,1)S(1)} %collective-permute-done), channel_id=1, source_target_pairs={{0,1},{1,2},{2,3},{3,0},{4,5},{5,6},{6,7},{7,4},{8,9},{9,10},{10,1... | collective-permute-start | bytes 1572872 | tf_op jit(solution)/shard_map/ppermute | solution.py:11
  22.6 3.6 %collective-permute-done.1 = bf16[512,512]{1,0:T(8,128)(2,1)S(1)} collective-permute-done((bf16[512,512]{1,0:T(8,128)(2,1)S(1)}, bf16[512,512]{1,0:T(8,128)(2,1)S(1)}, u32[]{:S(2)}, u32[]{:S(2)}) %collective-permute-start.1) | collective-permute-done | bytes 524320 | tf_op jit(solution)/shard_map/ppermute | solution.py:11
  27.1 7.7 %collective-permute-done.2 = bf16[512,512]{1,0:T(8,128)(2,1)S(1)} collective-permute-done((bf16[512,512]{1,0:T(8,128)(2,1)S(1)}, bf16[512,512]{1,0:T(8,128)(2,1)S(1)}, u32[]{:S(2)}, u32[]{:S(2)}) %collective-permute-start.2) | collective-permute-done | bytes 524320 | tf_op jit(solution)/shard_map/ppermute | solution.py:11
  42.0 43.0 %all-gather.2.cloned.1.call-done = bf16[2048,1024]{1,0:T(8,128)(2,1)} async-done(((bf16[256,1024]{1,0:T(8,128)(2,1)}), bf16[2048,1024]{1,0:T(8,128)(2,1)}) %all-gather.2.cloned.1.call-update) | async-done | bytes 4194320 | tf_op jit(solution)/shard_map/all_gather | solution.py:39
  85.0 5.2 %fusion.6 = bf16[512,1024]{1,0:T(8,128)(2,1)S(1)} fusion(bf16[2048,1024]{1,0:T(8,128)(2,1)} %all-gather.2.cloned.1.call-done, bf16[512,4096]{1,0:T(8,128)(2,1)} %constant_dynamic-update-slice_fusion, s32[]{:T(128)S(6)} %select_n.82), kind=kOutput, calls=%fused_computation.10 | convolution fusion | flops 2148007936 | bytes 7340036 | tf_op jit(solution)/shard_map/dot_general | solution.py:37
  90.2 1.3 convolution_bitcast_fusion
  92.0 1.9 %fusion.34 = f32[4,128,1024]{1,2,0:T(8,128)} fusion(bf16[4,128,1024]{2,1,0:T(8,128)(2,1)S(1)} %bitcast.186, bf16[4,128,128]{2,1,0:T(8,128)(2,1)S(1)} %convolution_convert_fusion.1, pred[128,128]{1,0:T(8,128)(4,1)S(1)} %copy-done.11), kind=kOutput, calls=%fused_computation.50 | convolution fusion | flops 134283264 | bytes 3293184 | tf_op jit(solution)/shard_map/bij,bjc->bic/dot_general | solution.py:63
  93.9 1.8 %fusion.36 = f32[4,128,1024]{1,2,0:T(8,128)} fusion(bf16[4,128,1024]{2,1,0:T(8,128)(2,1)S(1)} %bitcast.187, bf16[4,128,128]{2,1,0:T(8,128)(2,1)S(1)} %convolution_convert_fusion.1, pred[128,128]{1,0:T(8,128)(4,1)S(1)} %copy-done.10), kind=kOutput, calls=%fused_computation.52 | convolution fusion | flops 134283264 | bytes 3293184 | tf_op jit(solution)/shard_map/bij,bjc->bic/dot_general | solution.py:63
  95.7 1.9 %fusion.38 = f32[4,128,1024]{1,2,0:T(8,128)} fusion(bf16[4,128,1024]{2,1,0:T(8,128)(2,1)S(1)} %bitcast.188, bf16[4,128,128]{2,1,0:T(8,128)(2,1)S(1)} %convolution_convert_fusion.1, pred[128,128]{1,0:T(8,128)(4,1)S(1)} %copy-done.9), kind=kOutput, calls=%fused_computation.54 | convolution fusion | flops 134283264 | bytes 3293184 | tf_op jit(solution)/shard_map/bij,bjc->bic/dot_general | solution.py:63
  97.6 1.9 %fusion.40 = f32[4,128,1024]{1,2,0:T(8,128)} fusion(bf16[4,128,1024]{2,1,0:T(8,128)(2,1)S(1)} %bitcast.189, bf16[4,128,128]{2,1,0:T(8,128)(2,1)S(1)} %convolution_convert_fusion.1, pred[128,128]{1,0:T(8,128)(4,1)S(1)} %copy-done.15), kind=kOutput, calls=%fused_computation.56 | convolution fusion | flops 134283264 | bytes 3293184 | tf_op jit(solution)/shard_map/bij,bjc->bic/dot_general | solution.py:63
  99.6 1.9 %fusion.42 = f32[4,128,1024]{1,2,0:T(8,128)} fusion(bf16[4,128,1024]{2,1,0:T(8,128)(2,1)S(1)} %bitcast.190, bf16[4,128,128]{2,1,0:T(8,128)(2,1)S(1)} %convolution_convert_fusion.1, pred[128,128]{1,0:T(8,128)(4,1)S(1)} %copy-done.14), kind=kOutput, calls=%fused_computation.58 | convolution fusion | flops 134283264 | bytes 3293184 | tf_op jit(solution)/shard_map/bij,bjc->bic/dot_general | solution.py:63
  101.5 1.9 %fusion.44 = f32[4,128,1024]{1,2,0:T(8,128)} fusion(bf16[4,128,1024]{2,1,0:T(8,128)(2,1)S(1)} %bitcast.191, bf16[4,128,128]{2,1,0:T(8,128)(2,1)S(1)} %convolution_convert_fusion.1, pred[128,128]{1,0:T(8,128)(4,1)S(1)} %copy-done.13), kind=kOutput, calls=%fused_computation.60 | convolution fusion | flops 134283264 | bytes 3293184 | tf_op jit(solution)/shard_map/bij,bjc->bic/dot_general | solution.py:63
  103.4 1.8 %fusion.46 = f32[4,128,1024]{1,2,0:T(8,128)} fusion(bf16[4,128,1024]{2,1,0:T(8,128)(2,1)S(1)} %bitcast.192, bf16[4,128,128]{2,1,0:T(8,128)(2,1)S(1)} %convolution_convert_fusion.1, pred[128,128]{1,0:T(8,128)(4,1)S(1)} %copy-done.16), kind=kOutput, calls=%fused_computation.62 | convolution fusion | flops 134283264 | bytes 3293184 | tf_op jit(solution)/shard_map/bij,bjc->bic/dot_general | solution.py:63
  105.3 1.4 fusion.13
  106.7 7.9 %multiply_add_fusion = f32[2,2,128,16,64]{2,4,3,1,0:T(8,128)S(1)} fusion(f32[2,2,128,16,64]{2,4,3,1,0:T(8,128)S(1)} %bitcast.198, f32[2,2,128,16,64]{2,4,3,1,0:T(8,128)} %bitcast.199, f32[2,2,128,16,64]{2,4,3,1,0:T(8,128)} %bitcast.200, f32[2,2,128,16,64]{2,4,3,1,0:T(8,128)} %bitcast.201, f32[2,2,128,16,64]{2,4,3,1,0:T(8,128)} %bitcast.202, ...), kind=kLoop, calls=%fused_computation.7 | loop fusion | flops 7864320 | bytes 19136512 | tf_op jit(solution)/shard_map/add | solution.py:65
  114.9 3.2 %copy.41 = f32[2,2,128,16,64]{2,1,4,3,0:T(2,128)} copy(f32[2,2,128,16,64]{2,4,3,1,0:T(8,128)S(1)} %fusion.14) | data formatting | bytes 4194304 | tf_op jit(solution)/shard_map/scatter-add | solution.py:79
  118.1 2.9 %reshape_reshape.3 = f32[1,2,256,16,64]{2,4,3,1,0:T(8,128)S(1)} reshape(f32[2,2,128,16,64]{2,1,4,3,0:T(2,128)} %copy.41) | data formatting | bytes 4194304 | tf_op jit(solution)/shard_map/reshape;reshape | solution.py:79
  124.2 1.6 copy.44
  126.1 7.8 %collective-permute-done.3 = f32[128,1024]{0,1:T(8,128)} collective-permute-done((f32[128,1024]{0,1:T(8,128)}, f32[128,1024]{0,1:T(8,128)}, u32[]{:S(2)}, u32[]{:S(2)}) %collective-permute-start.3) | collective-permute-done | bytes 524320 | tf_op jit(solution)/shard_map/ppermute | solution.py:24
  136.6 10.0 %collective-permute-done.4 = f32[128,1024]{0,1:T(8,128)S(1)} collective-permute-done((f32[128,1024]{0,1:T(8,128)S(1)}, f32[128,1024]{0,1:T(8,128)S(1)}, u32[]{:S(2)}, u32[]{:S(2)}) %collective-permute-start.4) | collective-permute-done | bytes 524320 | tf_op jit(solution)/shard_map/ppermute | solution.py:24
  146.7 3.0 %collective-permute-start.5 = (f32[128,1024]{0,1:T(8,128)S(1)}, f32[128,1024]{0,1:T(8,128)S(1)}, u32[]{:S(2)}, u32[]{:S(2)}) collective-permute-start(f32[128,1024]{0,1:T(8,128)S(1)} %add.384), channel_id=1, source_target_pairs={{0,16},{16,0},{4,20},{20,4},{8,24},{24,8},{12,28},{28,12},{1,17},{... | collective-permute-start | bytes 1572872 | tf_op jit(solution)/shard_map/ppermute | solution.py:24
  150.6 20.2 %collective-permute-done.5 = f32[128,1024]{0,1:T(8,128)S(1)} collective-permute-done((f32[128,1024]{0,1:T(8,128)S(1)}, f32[128,1024]{0,1:T(8,128)S(1)}, u32[]{:S(2)}, u32[]{:S(2)}) %collective-permute-start.5) | collective-permute-done | bytes 524320 | tf_op jit(solution)/shard_map/ppermute | solution.py:24
  172.0 1.3 copy.45
  (94 shorter events, 29.0 us)
Async XLA Ops:
  6.5 20.4 %copy-start = (bf16[512,128]{1,0:T(8,128)(2,1)S(1)}, bf16[512,128]{1,0:T(8,128)(2,1)}, u32[]{:S(2)}) copy-start(bf16[512,128]{1,0:T(8,128)(2,1)} %param.11) | copy-start | bytes 393220
  6.5 20.4 %copy-start.4 = (bf16[512,128]{1,0:T(8,128)(2,1)S(1)}, bf16[512,128]{1,0:T(8,128)(2,1)}, u32[]{:S(2)}) copy-start(bf16[512,128]{1,0:T(8,128)(2,1)} %param.12) | copy-start | bytes 393220
  6.5 78.5 %all-gather.2.cloned.1.call-start = ((), (), s32[]{:S(2)}) async-start(), calls=%async_computation | async-start | bytes 4718592 | tf_op jit(solution)/shard_map/all_gather | solution.py:39
  7.3 10.2 %collective-permute-start = (bf16[512,512]{1,0:T(8,128)(2,1)}, bf16[512,512]{1,0:T(8,128)(2,1)S(1)}, u32[]{:S(2)}, u32[]{:S(2)}) collective-permute-start(bf16[512,512]{1,0:T(8,128)(2,1)} %param.9), channel_id=1, source_target_pairs={{0,1},{1,2},{2,3},{3,0},{4,5},{5,6},{6,7},{7,4},{8,9},{9,10},{10,1... | collective-permute-start | bytes 1572872 | tf_op jit(solution)/shard_map/ppermute | solution.py:11
  13.3 24.4 %copy-start.3 = (bf16[512,512]{1,0:T(8,128)(2,1)S(1)}, bf16[512,512]{1,0:T(8,128)(2,1)}, u32[]{:S(2)}) copy-start(bf16[512,512]{1,0:T(8,128)(2,1)} %param.9) | copy-start | bytes 1572868
  17.4 8.8 %collective-permute-start.1 = (bf16[512,512]{1,0:T(8,128)(2,1)S(1)}, bf16[512,512]{1,0:T(8,128)(2,1)S(1)}, u32[]{:S(2)}, u32[]{:S(2)}) collective-permute-start(bf16[512,512]{1,0:T(8,128)(2,1)S(1)} %collective-permute-done), channel_id=1, source_target_pairs={{0,1},{1,2},{2,3},{3,0},{4,5},{5,6},{6,7},{7,4},{8,9},{9,10},{10,1... | collective-permute-start | bytes 1572872 | tf_op jit(solution)/shard_map/ppermute | solution.py:11
  26.2 8.6 %collective-permute-start.2 = (bf16[512,512]{1,0:T(8,128)(2,1)S(1)}, bf16[512,512]{1,0:T(8,128)(2,1)S(1)}, u32[]{:S(2)}, u32[]{:S(2)}) collective-permute-start(bf16[512,512]{1,0:T(8,128)(2,1)S(1)} %collective-permute-done.1), channel_id=1, source_target_pairs={{0,1},{1,2},{2,3},{3,0},{4,5},{5,6},{6,7},{7,4},{8,9},{9,10},{10,1... | collective-permute-start | bytes 1572872 | tf_op jit(solution)/shard_map/ppermute | solution.py:11
  85.0 6.5 %copy-start.12 = (pred[128,128]{1,0:T(8,128)(4,1)S(1)}, pred[128,128]{1,0:T(8,128)(4,1)}, u32[]{:S(2)}) copy-start(pred[128,128]{1,0:T(8,128)(4,1)} %fusion.63) | copy-start | bytes 49156
  90.2 1.8 %copy-start.11 = (pred[128,128]{1,0:T(8,128)(4,1)S(1)}, pred[128,128]{1,0:T(8,128)(4,1)}, u32[]{:S(2)}) copy-start(pred[128,128]{1,0:T(8,128)(4,1)} %fusion.64) | copy-start | bytes 49156
  92.0 1.9 %copy-start.10 = (pred[128,128]{1,0:T(8,128)(4,1)S(1)}, pred[128,128]{1,0:T(8,128)(4,1)}, u32[]{:S(2)}) copy-start(pred[128,128]{1,0:T(8,128)(4,1)} %fusion.65) | copy-start | bytes 49156
  93.9 1.8 %copy-start.9 = (pred[128,128]{1,0:T(8,128)(4,1)S(1)}, pred[128,128]{1,0:T(8,128)(4,1)}, u32[]{:S(2)}) copy-start(pred[128,128]{1,0:T(8,128)(4,1)} %fusion.66) | copy-start | bytes 49156
  95.7 1.9 %copy-start.15 = (pred[128,128]{1,0:T(8,128)(4,1)S(1)}, pred[128,128]{1,0:T(8,128)(4,1)}, u32[]{:S(2)}) copy-start(pred[128,128]{1,0:T(8,128)(4,1)} %fusion.67) | copy-start | bytes 49156
  97.6 1.9 %copy-start.14 = (pred[128,128]{1,0:T(8,128)(4,1)S(1)}, pred[128,128]{1,0:T(8,128)(4,1)}, u32[]{:S(2)}) copy-start(pred[128,128]{1,0:T(8,128)(4,1)} %fusion.68) | copy-start | bytes 49156
  99.6 1.9 %copy-start.13 = (pred[128,128]{1,0:T(8,128)(4,1)S(1)}, pred[128,128]{1,0:T(8,128)(4,1)}, u32[]{:S(2)}) copy-start(pred[128,128]{1,0:T(8,128)(4,1)} %fusion.69) | copy-start | bytes 49156
  101.5 1.9 %copy-start.16 = (pred[128,128]{1,0:T(8,128)(4,1)S(1)}, pred[128,128]{1,0:T(8,128)(4,1)}, u32[]{:S(2)}) copy-start(pred[128,128]{1,0:T(8,128)(4,1)} %fusion.70) | copy-start | bytes 49156
  106.7 7.9 %copy-start.1 = (f32[2,128,1024]{1,2,0:T(8,128)S(1)}, f32[2,128,1024]{1,2,0:T(8,128)}, u32[]{:S(2)}) copy-start(f32[2,128,1024]{1,2,0:T(8,128)} %fusion.13) | copy-start | bytes 3145732
  106.7 7.9 %copy-start.8 = (f32[2,128,16]{1,2,0:T(8,128)S(1)}, f32[2,128,16]{1,2,0:T(8,128)}, u32[]{:S(2)}) copy-start(f32[2,128,16]{1,2,0:T(8,128)} %fusion.87) | copy-start | bytes 49156
  121.0 12.8 %collective-permute-start.3 = (f32[128,1024]{0,1:T(8,128)}, f32[128,1024]{0,1:T(8,128)}, u32[]{:S(2)}, u32[]{:S(2)}) collective-permute-start(f32[128,1024]{0,1:T(8,128)} %convolution_bitcast_fusion), channel_id=1, source_target_pairs={{0,4},{4,0},{8,12},{12,8},{16,20},{20,16},{24,28},{28,24},{1,5},{5... | collective-permute-start | bytes 1572872 | tf_op jit(solution)/shard_map/ppermute | solution.py:24
  125.9 8.0 %copy-start.2 = (f32[128,1024]{0,1:T(8,128)S(1)}, f32[128,1024]{0,1:T(8,128)}, u32[]{:S(2)}) copy-start(f32[128,1024]{0,1:T(8,128)} %convolution_bitcast_fusion) | copy-start | bytes 1572868
  135.0 11.6 %collective-permute-start.4 = (f32[128,1024]{0,1:T(8,128)S(1)}, f32[128,1024]{0,1:T(8,128)S(1)}, u32[]{:S(2)}, u32[]{:S(2)}) collective-permute-start(f32[128,1024]{0,1:T(8,128)S(1)} %add.379), channel_id=1, source_target_pairs={{0,8},{8,0},{4,12},{12,4},{16,24},{24,16},{20,28},{28,20},{1,9},{9... | collective-permute-start | bytes 1572872 | tf_op jit(solution)/shard_map/ppermute | solution.py:24
  146.7 24.1 %collective-permute-start.5 = (f32[128,1024]{0,1:T(8,128)S(1)}, f32[128,1024]{0,1:T(8,128)S(1)}, u32[]{:S(2)}, u32[]{:S(2)}) collective-permute-start(f32[128,1024]{0,1:T(8,128)S(1)} %add.384), channel_id=1, source_target_pairs={{0,16},{16,0},{4,20},{20,4},{8,24},{24,8},{12,28},{28,12},{1,17},{... | collective-permute-start | bytes 1572872 | tf_op jit(solution)/shard_map/ppermute | solution.py:24
  150.1 21.1 %copy-start.5 = (f32[512,16]{0,1:T(8,128)S(1)}, f32[512,16]{0,1:T(8,128)}, u32[]{:S(2)}) copy-start(f32[512,16]{0,1:T(8,128)} %get-tuple-element.29) | copy-start | bytes 98308
  150.1 21.1 %copy-start.6 = (f32[512,16]{0,1:T(8,128)S(1)}, f32[512,16]{0,1:T(8,128)}, u32[]{:S(2)}) copy-start(f32[512,16]{0,1:T(8,128)} %get-tuple-element.40) | copy-start | bytes 98308
  150.1 21.1 %copy-start.7 = (f32[512,16]{0,1:T(8,128)S(1)}, f32[512,16]{0,1:T(8,128)}, u32[]{:S(2)}) copy-start(f32[512,16]{0,1:T(8,128)} %get-tuple-element.41) | copy-start | bytes 98308
Sparse Core Ops, SparseCore 0:
  9.5 75.5 all-gather.1
